TPU v7x, 128 devices: a whole 4x4x4 slice. The times are simulated.
128 devices in a mesh: seq: 32 (over z, x, core), batch: 4 (over y).
Axes of the slice: x: 4, y: 4, z: 4, core: 2. Of those that a mesh axis runs over, the one named last changes fastest.
Arguments:
- sequence_input: bfloat16 [32768, 1536], P(('batch', 'seq')), parts along dimension 0, may hold values from -6 to 6
- conv_first: bfloat16 [5, 1536, 768], replicated, may hold values from -0.0625 to 0.0625
- conv_second: bfloat16 [5, 768, 768], replicated, may hold values from -0.09375 to 0.09375
- qkv_weight: bfloat16 [768, 1536], replicated, may hold values from -0.21875 to 0.21875
- out_weight: bfloat16 [512, 768], replicated, may hold values from -0.25 to 0.25
- logit_scale: float32 [4], replicated, may hold values from 2.5 to 30, as said below
Outputs:
- block_output: bfloat16 [32768, 768], P(('batch', 'seq')), parts along dimension 0
There are 4 independent parts, one for each index of `batch`. A program takes and returns all parts, laid end to end along the dimension named above; an argument that names none is the same for every part. Nothing has to cross between parts.
Inputs may be any that keep to these rules, and one draw needn't show every extreme that they name: `logit_scale`: one positive scale a head.
All inputs are finite; a program needn't handle non-finite values.
Results may differ from a plain program's by a relative error of at most 0.023.
Values may be sent and summed in bfloat16 or wider, within the bound.
A program may use at most 256 MiB of HBM per device.

v0:
```python
import math
import jax
import jax.numpy as jnp
from jax import lax
from jax.sharding import PartitionSpec as P


def padded_2(block, sides, width):
    for axis, dim in sides:
        count = lax.axis_size(axis)
        forward = [(i, i + 1) for i in range(count - 1)]
        backward = [(target, source) for source, target in forward]
        low = lax.ppermute(
            lax.slice_in_dim(block, block.shape[dim] - width, None, axis=dim), axis, forward
        )
        high = lax.ppermute(lax.slice_in_dim(block, 0, width, axis=dim), axis, backward)
        block = jnp.concatenate([low, block, high], axis=dim)
    return block


def convolve(padded, weight, row_count):
    conv_sum = jnp.dot(padded[0:row_count], weight[0], preferred_element_type=jnp.float32)
    for offset in range(1, weight.shape[0]):
        conv_sum = conv_sum + jnp.dot(
            padded[offset : offset + row_count], weight[offset], preferred_element_type=jnp.float32
        )
    return conv_sum


def head_rms(tensor):
    return tensor * lax.rsqrt(jnp.mean(tensor * tensor, axis=-1, keepdims=True) + 1e-06)


def attend_block(state_now, queries, key_block, value_block):
    running_max, running_sum, running_out = state_now
    scores = jnp.einsum("thd,shd->hts", queries, key_block, preferred_element_type=jnp.float32)
    new_max = jnp.maximum(running_max, jnp.max(scores, axis=2))
    weights = jnp.exp(scores - new_max[:, :, None])
    running_sum = jnp.sum(weights, axis=2)
    running_out = jnp.einsum(
        "hts,shd->htd",
        weights.astype(jnp.bfloat16),
        value_block,
        preferred_element_type=jnp.float32,
    )
    return (new_max, running_sum, running_out)


def body(sequence_input, conv_first, conv_second, qkv_weight, out_weight, logit_scale):
    row_count = sequence_input.shape[0]
    padded_input = padded_2(sequence_input, (("seq", 0),), 2)
    first_out = jax.nn.gelu(convolve(padded_input, conv_first, row_count)).astype(jnp.bfloat16)
    padded_first = padded_2(first_out, (("seq", 0),), 2)
    second = convolve(padded_first, conv_second, row_count)
    hidden = (first_out.astype(jnp.float32) + second).astype(jnp.bfloat16)
    head_count = logit_scale.shape[0]
    width_all = qkv_weight.shape[1] // 3
    head_size = width_all // head_count
    query_part = jnp.dot(hidden, qkv_weight[:, :width_all], preferred_element_type=jnp.float32)
    query_part = query_part.reshape(row_count, head_count, head_size)
    queries = (head_rms(query_part) * (logit_scale / math.sqrt(head_size))[None, :, None]).astype(
        jnp.bfloat16
    )
    kv_weight = qkv_weight[:, width_all:]
    start_state = (
        jnp.full((head_count, row_count), -1e30, jnp.float32),
        jnp.zeros((head_count, row_count), jnp.float32),
        jnp.zeros((head_count, row_count, head_size), jnp.float32),
    )
    piece_rows = hidden.shape[0]
    paired = jnp.dot(hidden, kv_weight, preferred_element_type=jnp.float32)
    key_block = head_rms(paired[:, :width_all].reshape(piece_rows, head_count, head_size)).astype(
        jnp.bfloat16
    )
    value_block = (
        paired[:, width_all:].reshape(piece_rows, head_count, head_size).astype(jnp.bfloat16)
    )
    own_keys = key_block
    own_values = value_block
    flat_keys = own_keys.reshape(row_count, width_all)
    flat_values = own_values.reshape(row_count, width_all)
    piece_pair = (
        lax.all_gather(flat_keys, "seq", axis=0, tiled=True),
        lax.all_gather(flat_values, "seq", axis=0, tiled=True),
    )
    piece_rows = piece_pair[0].shape[0]
    key_block = piece_pair[0].reshape(piece_rows, head_count, head_size)
    value_block = piece_pair[1].reshape(piece_rows, head_count, head_size)
    final_state = attend_block(start_state, queries, key_block, value_block)
    running_max, running_sum, running_out = final_state
    attended = (
        (running_out / running_sum[:, :, None])
        .transpose(1, 0, 2)
        .reshape(row_count, width_all)
        .astype(jnp.bfloat16)
    )
    return (
        hidden.astype(jnp.float32)
        + jnp.dot(attended, out_weight, preferred_element_type=jnp.float32)
    ).astype(jnp.bfloat16)


def solution(mesh):
    in_specs = (P(("batch", "seq"), None), P(), P(), P(), P(), P())
    out_specs = P(("batch", "seq"), None)
    return jax.shard_map(body, mesh=mesh, in_specs=in_specs, out_specs=out_specs, check_vma=False)
```

profile of v0, /device:TPU:1, one launch (start us, length us, event | category | flops | bytes accessed | tf_op | source)
XLA Modules:
  0.0 185.4 jit_solution(1731052009252895028)
XLA Ops:
  6.5 0.0 copy-start
  6.5 0.0 all-gather.3.cloned.1.call-start
  6.5 0.8 fusion.101
  7.4 3.3 %collective-permute-start.1 = (bf16[2,1536]{1,0:T(2,128)(2,1)S(1)}, bf16[2,1536]{1,0:T(2,128)(2,1)S(1)}, u32[]{:S(2)}, u32[]{:S(2)}) collective-permute-start(bf16[2,1536]{1,0:T(2,128)(2,1)S(1)} %get-tuple-element.6), channel_id=1, source_target_pairs={{4,0},{8,4},{12,8},{16,12},{20,16},{24,20},{28,24},{32,28},{36,32}... | collective-permute-start | bytes 18440 | tf_op jit(solution)/shard_map/ppermute | solution.py:16
  10.7 0.0 copy-start.3
  10.7 3.5 %collective-permute-start = (bf16[2,1536]{1,0:T(2,128)(2,1)S(1)}, bf16[2,1536]{1,0:T(2,128)(2,1)S(1)}, u32[]{:S(2)}, u32[]{:S(2)}) collective-permute-start(bf16[2,1536]{1,0:T(2,128)(2,1)S(1)} %get-tuple-element.5), channel_id=1, source_target_pairs={{0,4},{4,8},{8,12},{12,16},{16,20},{20,24},{24,28},{28,32},{32,36}... | collective-permute-start | bytes 18440 | tf_op jit(solution)/shard_map/ppermute | solution.py:13
  14.2 2.7 %fusion.12 = f32[256,768]{1,0:T(8,128)S(1)} fusion(bf16[256,1536]{1,0:T(8,128)(2,1)} %param.6, bf16[5,1536,768]{2,1,0:T(8,128)(2,1)} %param.7), kind=kOutput, calls=%fused_computation.12 | convolution fusion | flops 603979776 | bytes 3932160 | tf_op jit(solution)/shard_map/dot_general | solution.py:24
  16.9 1.2 constant_dynamic-update-slice_fusion.1
  18.1 0.0 copy-start.2
  18.1 0.0 collective-permute-done.1
  18.2 2.5 %fusion.8 = f32[256,768]{1,0:T(8,128)S(1)} fusion(bf16[5,1536,768]{2,1,0:T(8,128)(2,1)} %param.7, bf16[258,1536]{1,0:T(8,128)(2,1)S(1)} %constant_dynamic-update-slice_fusion), kind=kOutput, calls=%fused_computation.8 | convolution fusion | flops 603979776 | bytes 3932160 | tf_op jit(solution)/shard_map/dot_general | solution.py:24
  20.7 0.0 copy-done.3
  20.7 0.8 fusion.10
  21.5 0.0 slice-start
  21.5 0.0 collective-permute-done
  21.5 0.0 copy-done.2
  21.5 0.8 fusion.14
  22.4 0.0 slice-start.1
  22.4 1.0 fusion.77
  23.4 2.9 %collective-permute-start.2 = (bf16[2,768]{1,0:T(2,128)(2,1)S(1)}, bf16[2,768]{1,0:T(2,128)(2,1)S(1)}, u32[]{:S(2)}, u32[]{:S(2)}) collective-permute-start(bf16[2,768]{1,0:T(2,128)(2,1)S(1)} %get-tuple-element.7), channel_id=1, source_target_pairs={{0,4},{4,8},{8,12},{12,16},{16,20},{20,24},{24,28},{28,32},{32,36}... | collective-permute-start | bytes 9224 | tf_op jit(solution)/shard_map/ppermute | solution.py:13
  26.3 0.0 slice-done
  26.3 0.0 slice-done.1
  26.4 0.5 fusion.54
  26.8 1.9 %collective-permute-start.3 = (bf16[2,768]{1,0:T(2,128)(2,1)S(1)}, bf16[2,768]{1,0:T(2,128)(2,1)S(1)}, u32[]{:S(2)}, u32[]{:S(2)}) collective-permute-start(bf16[2,768]{1,0:T(2,128)(2,1)S(1)} %get-tuple-element.8), channel_id=1, source_target_pairs={{4,0},{8,4},{12,8},{16,12},{20,16},{24,20},{28,24},{32,28},{36,32}... | collective-permute-start | bytes 9224 | tf_op jit(solution)/shard_map/ppermute | solution.py:16
  28.8 0.0 collective-permute-done.2
  28.8 0.5 fusion.56
  29.3 0.0 copy-start.1
  29.3 2.5 %collective-permute-done.3 = bf16[2,768]{1,0:T(2,128)(2,1)S(1)} collective-permute-done((bf16[2,768]{1,0:T(2,128)(2,1)S(1)}, bf16[2,768]{1,0:T(2,128)(2,1)S(1)}, u32[]{:S(2)}, u32[]{:S(2)}) %collective-permute-start.3) | collective-permute-done | bytes 3104 | tf_op jit(solution)/shard_map/ppermute | solution.py:16
  31.8 0.5 fusion.51
  32.2 0.5 fusion.33
  32.8 0.0 copy-start.4
  32.8 0.5 fusion.40
  33.3 0.0 copy-done.1
  33.3 0.6 fusion.23
  33.9 0.2 mul.70
  34.1 0.3 reduce_sum.28
  34.5 0.3 mul.71
  34.9 0.8 fusion.87
  35.6 0.0 all-gather.3.cloned.1.call-update
  35.7 0.2 all-gather.5.cloned.1.call-start
  35.9 0.7 slice.220
  36.6 0.0 all-gather.5.cloned.1.call-update
  36.7 0.0 copy-done.4
  36.7 1.5 fusion.85
  38.2 0.2 reshape.38
  38.4 0.3 multiply_reduce_fusion
  38.8 0.3 multiply_convert_fusion
  39.1 55.5 %all-gather.3.cloned.1.call-done = bf16[8192,512]{1,0:T(8,128)(2,1)} async-done(((bf16[256,512]{1,0:T(8,128)(2,1)}), bf16[8192,512]{1,0:T(8,128)(2,1)}) %all-gather.3.cloned.1.call-update) | async-done | bytes 8388624 | tf_op jit(solution)/shard_map/all_gather | solution.py:83
  94.6 16.8 %fusion.103 = (f32[4,256]{1,0:T(4,128)S(1)}, f32[4,256,8192]{2,1,0:T(8,128)}) fusion(bf16[256,4,128]{2,1,0:T(4,128)(2,1)S(1)} %multiply_convert_fusion, bf16[8192,512]{1,0:T(8,128)(2,1)} %all-gather.3.cloned.1.call-done), kind=kOutput, calls=%fused_computation.102 | convolution fusion | flops 2155871232 | bytes 42209280 | tf_op jit(solution)/shard_map/thd,shd->hts/dot_general | solution.py:36
  111.4 13.7 %fusion = f32[4,256]{1,0:T(4,128)S(1)} fusion(f32[4,256,8192]{2,1,0:T(8,128)} %get-tuple-element.10, f32[4,256]{1,0:T(4,128)S(1)} %broadcast_maximum_fusion), kind=kLoop, calls=%fused_computation.1 | loop fusion | flops 16776192 | bytes 33562624 | tf_op jit(solution)/shard_map/reduce_sum | solution.py:39
  125.2 24.3 %all-gather.5.cloned.1.call-done = bf16[8192,512]{1,0:T(8,128)(2,1)} async-done(((bf16[256,512]{1,0:T(8,128)(2,1)}), bf16[8192,512]{1,0:T(8,128)(2,1)}) %all-gather.5.cloned.1.call-update) | async-done | bytes 8388624 | tf_op jit(solution)/shard_map/all_gather | solution.py:84
  149.4 12.0 %copy.21 = bf16[8192,512]{0,1:T(8,128)(2,1)} copy(bf16[8192,512]{1,0:T(8,128)(2,1)} %all-gather.5.cloned.1.call-done) | data formatting | bytes 16777216 | tf_op jit(solution)/shard_map/reshape | solution.py:88
  161.4 16.0 %fusion.48 = bf16[256,4,128]{0,2,1:T(8,128)(2,1)S(1)} fusion(bf16[8192,4,128]{0,2,1:T(8,128)(2,1)} %bitcast.72, f32[4,256,8192]{2,1,0:T(8,128)} %get-tuple-element.10, f32[4,256]{1,0:T(4,128)S(1)} %broadcast_maximum_fusion, f32[256,4]{0,1:T(4,128)S(1)} %bitcast.77), kind=kOutput, calls=%fused_computation.39 | convolution fusion | flops 2164523008 | bytes 42213376 | tf_op jit(solution)/shard_map/hts,shd->htd/dot_general | solution.py:40
  177.4 0.0 copy-done
  177.5 1.1 fusion.41
  (8 shorter events, 0.1 us)
Async XLA Ops:
  6.5 170.9 %copy-start = (bf16[512,768]{1,0:T(8,128)(2,1)S(1)}, bf16[512,768]{1,0:T(8,128)(2,1)}, u32[]{:S(2)}) copy-start(bf16[512,768]{1,0:T(8,128)(2,1)} %param.10) | copy-start | bytes 2359300
  6.5 88.1 %all-gather.3.cloned.1.call-start = ((), (), s32[]{:S(2)}) async-start(), calls=%async_computation | async-start | bytes 8650752 | tf_op jit(solution)/shard_map/all_gather | solution.py:83
  7.4 10.8 %collective-permute-start.1 = (bf16[2,1536]{1,0:T(2,128)(2,1)S(1)}, bf16[2,1536]{1,0:T(2,128)(2,1)S(1)}, u32[]{:S(2)}, u32[]{:S(2)}) collective-permute-start(bf16[2,1536]{1,0:T(2,128)(2,1)S(1)} %get-tuple-element.6), channel_id=1, source_target_pairs={{4,0},{8,4},{12,8},{16,12},{20,16},{24,20},{28,24},{32,28},{36,32}... | collective-permute-start | bytes 18440 | tf_op jit(solution)/shard_map/ppermute | solution.py:16
  10.7 10.0 %copy-start.3 = (bf16[5,1536,768]{2,1,0:T(8,128)(2,1)S(1)}, bf16[5,1536,768]{2,1,0:T(8,128)(2,1)}, u32[]{:S(2)}) copy-start(bf16[5,1536,768]{2,1,0:T(8,128)(2,1)} %param.7) | copy-start | bytes 35389444
  10.7 10.8 %collective-permute-start = (bf16[2,1536]{1,0:T(2,128)(2,1)S(1)}, bf16[2,1536]{1,0:T(2,128)(2,1)S(1)}, u32[]{:S(2)}, u32[]{:S(2)}) collective-permute-start(bf16[2,1536]{1,0:T(2,128)(2,1)S(1)} %get-tuple-element.5), channel_id=1, source_target_pairs={{0,4},{4,8},{8,12},{12,16},{16,20},{20,24},{24,28},{28,32},{32,36}... | collective-permute-start | bytes 18440 | tf_op jit(solution)/shard_map/ppermute | solution.py:13
  18.1 3.4 %copy-start.2 = (bf16[256,1536]{1,0:T(8,128)(2,1)S(1)}, bf16[256,1536]{1,0:T(8,128)(2,1)}, u32[]{:S(2)}) copy-start(bf16[256,1536]{1,0:T(8,128)(2,1)} %param.6) | copy-start | bytes 2359300
  21.5 4.8 %slice-start = ((s8[5898240]{0:T(1024)(128)(4,1)}), s8[4194304]{0:T(1024)(128)(4,1)S(1)}, s32[]{:S(2)}) async-start(s8[5898240]{0:T(1024)(128)(4,1)} %bitcast.73), calls=%async_computation.2 | async-start | bytes 8388608
  22.4 4.0 %slice-start.1 = ((s8[5898240]{0:T(1024)(128)(4,1)}), s8[1703936]{0:T(1024)(128)(4,1)S(1)}, s32[]{:S(2)}) async-start(s8[5898240]{0:T(1024)(128)(4,1)} %bitcast.73), calls=%async_computation.3 | async-start | bytes 3407872
  23.4 5.4 %collective-permute-start.2 = (bf16[2,768]{1,0:T(2,128)(2,1)S(1)}, bf16[2,768]{1,0:T(2,128)(2,1)S(1)}, u32[]{:S(2)}, u32[]{:S(2)}) collective-permute-start(bf16[2,768]{1,0:T(2,128)(2,1)S(1)} %get-tuple-element.7), channel_id=1, source_target_pairs={{0,4},{4,8},{8,12},{12,16},{16,20},{20,24},{24,28},{28,32},{32,36}... | collective-permute-start | bytes 9224 | tf_op jit(solution)/shard_map/ppermute | solution.py:13
  26.8 4.9 %collective-permute-start.3 = (bf16[2,768]{1,0:T(2,128)(2,1)S(1)}, bf16[2,768]{1,0:T(2,128)(2,1)S(1)}, u32[]{:S(2)}, u32[]{:S(2)}) collective-permute-start(bf16[2,768]{1,0:T(2,128)(2,1)S(1)} %get-tuple-element.8), channel_id=1, source_target_pairs={{4,0},{8,4},{12,8},{16,12},{20,16},{24,20},{28,24},{32,28},{36,32}... | collective-permute-start | bytes 9224 | tf_op jit(solution)/shard_map/ppermute | solution.py:16
  29.3 4.0 %copy-start.1 = (bf16[768,1536]{1,0:T(8,128)(2,1)S(1)}, bf16[768,1536]{1,0:T(8,128)(2,1)}, u32[]{:S(2)}) copy-start(bf16[768,1536]{1,0:T(8,128)(2,1)} %param.9) | copy-start | bytes 7077892
  32.8 3.9 %copy-start.4 = (f32[4]{0:T(128)S(1)}, f32[4]{0:T(128)}, u32[]{:S(2)}) copy-start(f32[4]{0:T(128)} %param.11) | copy-start | bytes 52
  35.7 113.8 %all-gather.5.cloned.1.call-start = ((), (), s32[]{:S(2)}) async-start(), calls=%async_computation.1 | async-start | bytes 8650752 | tf_op jit(solution)/shard_map/all_gather | solution.py:84
Sparse Core Ops, SparseCore 0:
  35.8 58.7 all-gather.2
  96.9 52.5 all-gather.4
where the time goes:
time: 186 us; the launch traced here: 185 us
  waiting for transfers between devices  82.3 us (44%)
  matrix products  46.4 us (25%)
  other arithmetic  15.6 us (8%)
  local copies, waits for them, and re-layouts  15.5 us (8%)
  between operations  13.8 us (7%)
  starting transfers between devices  11.9 us (6%)
    all_gather x1, waiting for transfers between devices, body(): lax.all_gather(flat_keys, 'seq', axis=0, tiled=True)  55.5 us
    all_gather x1, waiting for transfers between devices, body(): lax.all_gather(flat_values, 'seq', axis=0, tiled=True)  24.3 us
    dot_general x1, matrix products, attend_block(): jnp.einsum('thd,shd->hts', queries, key_block, preferred_element_type=jnp...  16.8 us
    dot_general x1, matrix products, attend_block(): jnp.einsum('hts,shd->htd', weights.astype(jnp.bfloat16), value_block, pre...  16 us
    reduce_sum x1, other arithmetic, attend_block(): running_sum = jnp.sum(weights, axis=2)  13.7 us
    reshape x1, local copies, waits for them, and re-layouts, body(): value_block = piece_pair[1].reshape(piece_rows, head_count, head_size)  12 us
    dot_general x8, matrix products, convolve(): jnp.dot(padded[offset:offset + row_count], weight[offset], preferred_elem...  8.8 us
    ppermute x2, starting transfers between devices, padded_2(): lax.ppermute(lax.slice_in_dim(block, block.shape[dim] - width, None, axis...  6.42 us
  transfers between devices with their start and end apart: 6, of which 3 were waited for; matrix products, arithmetic and copies ran while one was open for 23% of the time, Pallas kernels for 0%

commit v1 on v0

--- a/solution.py
+++ b/solution.py
@@ -79,8 +79,17 @@
     own_values = value_block
     flat_keys = own_keys.reshape(row_count, width_all)
     flat_values = own_values.reshape(row_count, width_all)
+
+    def start_table_on(chip_axis, local_array):
+        n = lax.axis_size(chip_axis)
+        leaves = list(map(lambda b: n if b == 0 else 1, range(local_array.ndim)))
+        extra = lax.all_to_all(
+            jnp.tile(local_array, leaves), chip_axis, split_axis=0, concat_axis=0, tiled=True
+        )
+        return extra
+
     piece_pair = (
-        lax.all_gather(flat_keys, "seq", axis=0, tiled=True),
+        start_table_on("seq", flat_keys),
         lax.all_gather(flat_values, "seq", axis=0, tiled=True),
     )
     piece_rows = piece_pair[0].shape[0]

time: 186 us -> 263 us (1.41)
  the two profiles are of different devices: /device:TPU:1 before, /device:TPU:0 now
where the time goes in v1:
time: 263 us; the launch traced here: 262 us
  waiting for transfers between devices  120 us (46%)
  matrix products  46.1 us (18%)
  local copies, waits for them, and re-layouts  44.7 us (17%)
  starting transfers between devices  23.2 us (9%)
  other arithmetic  14.9 us (6%)
  between operations  13.8 us (5%)
    all_to_all x1, waiting for transfers between devices, start_table_on(): lax.all_to_all(jnp.tile(local_array, leaves), chip_axis, split_axis=0, co...  118 us
    dot_general x1, matrix products, attend_block(): jnp.einsum('thd,shd->hts', queries, key_block, preferred_element_type=jnp...  16.5 us
    dot_general x1, matrix products, attend_block(): jnp.einsum('hts,shd->htd', weights.astype(jnp.bfloat16), value_block, pre...  16 us
    all_to_all x1, starting transfers between devices, start_table_on(): lax.all_to_all(jnp.tile(local_array, leaves), chip_axis, split_axis=0, co...  14.1 us
    reduce_sum x1, other arithmetic, attend_block(): running_sum = jnp.sum(weights, axis=2)  13.6 us
    reshape x1, local copies, waits for them, and re-layouts, body(): key_block = piece_pair[0].reshape(piece_rows, head_count, head_size)  13.4 us
    reshape x1, local copies, waits for them, and re-layouts, body(): value_block = piece_pair[1].reshape(piece_rows, head_count, head_size)  12 us
    all_to_all x1, local copies, waits for them, and re-layouts, start_table_on(): lax.all_to_all(jnp.tile(local_array, leaves), chip_axis, split_axis=0, co...  11.4 us
  transfers between devices with their start and end apart: 6, of which 2 were waited for; matrix products, arithmetic and copies ran while one was open for 27% of the time, Pallas kernels for 0%

profile of v1, /device:TPU:0, one launch (start us, length us, event | category | flops | bytes accessed | tf_op | source)
XLA Modules:
  0.0 262.2 jit_solution(4857593313068001192)
XLA Ops:
  6.5 0.0 copy-start
  6.5 0.0 all-gather.2.cloned.1.call-start
  6.5 0.8 fusion.99
  7.4 1.3 collective-permute-start.1
  8.7 0.0 copy-start.3
  8.7 3.4 %collective-permute-start = (bf16[2,1536]{1,0:T(2,128)(2,1)S(1)}, bf16[2,1536]{1,0:T(2,128)(2,1)S(1)}, u32[]{:S(2)}, u32[]{:S(2)}) collective-permute-start(bf16[2,1536]{1,0:T(2,128)(2,1)S(1)} %get-tuple-element.5), channel_id=1, source_target_pairs={{0,4},{4,8},{8,12},{12,16},{16,20},{20,24},{24,28},{28,32},{32,36}... | collective-permute-start | bytes 18440 | tf_op jit(solution)/shard_map/ppermute | solution.py:13
  12.1 2.7 %fusion.9 = f32[256,768]{1,0:T(8,128)S(1)} fusion(bf16[256,1536]{1,0:T(8,128)(2,1)} %param.6, bf16[5,1536,768]{2,1,0:T(8,128)(2,1)} %param.7), kind=kOutput, calls=%fused_computation.9 | convolution fusion | flops 603979776 | bytes 3932160 | tf_op jit(solution)/shard_map/dot_general | solution.py:24
  14.8 1.2 constant_dynamic-update-slice_fusion.1
  16.0 0.0 copy-start.2
  16.0 0.0 collective-permute-done.1
  16.1 2.5 fusion.5
  18.6 0.0 copy-done.3
  18.6 0.8 fusion.7
  19.4 0.0 slice-start
  19.4 0.0 collective-permute-done
  19.4 0.0 copy-done.2
  19.4 0.8 fusion.11
  20.2 0.0 slice-start.1
  20.3 1.0 fusion.74
  21.3 3.1 %collective-permute-start.2 = (bf16[2,768]{1,0:T(2,128)(2,1)S(1)}, bf16[2,768]{1,0:T(2,128)(2,1)S(1)}, u32[]{:S(2)}, u32[]{:S(2)}) collective-permute-start(bf16[2,768]{1,0:T(2,128)(2,1)S(1)} %get-tuple-element.7), channel_id=1, source_target_pairs={{0,4},{4,8},{8,12},{12,16},{16,20},{20,24},{24,28},{28,32},{32,36}... | collective-permute-start | bytes 9224 | tf_op jit(solution)/shard_map/ppermute | solution.py:13
  24.4 0.0 slice-done
  24.4 0.0 slice-done.1
  24.4 0.5 fusion.51
  24.9 1.3 collective-permute-start.3
  26.2 0.0 collective-permute-done.2
  26.2 0.5 fusion.53
  26.7 0.0 copy-start.1
  26.7 1.8 collective-permute-done.3
  28.5 0.5 fusion.48
  29.0 0.5 fusion.30
  29.5 0.5 fusion.37
  30.0 0.0 copy-done.1
  30.0 0.6 fusion.20
  30.6 0.7 slice.220
  31.3 0.0 all-gather.2.cloned.1.call-update
  31.4 0.2 mul.71
  31.6 0.3 reduce_sum.28
  32.0 0.3 mul.72
  32.3 0.1 fusion.84
  32.4 0.1 copy.24
  32.6 4.2 %tile.2 = bf16[32,256,512]{1,2,0:T(8,128)(2,1)} broadcast(bf16[256,512]{0,1:T(8,128)(2,1)S(1)} %copy.24), dimensions={1,2} | broadcast | bytes 8650752 | tf_op jit(solution)/shard_map/tile | solution.py:87
  36.7 0.0 copy-start.4
  36.7 14.1 %all-to-all-start = ((bf16[32,256,512]{1,2,0:T(8,128)(2,1)}), bf16[32,256,512]{1,2,0:T(8,128)(2,1)}, u32[]{:S(2)}, u32[]{:S(2)}) async-start(bf16[32,256,512]{1,2,0:T(8,128)(2,1)} %tile.2), calls=%async_computation | async-start | bytes 16777216 | tf_op jit(solution)/shard_map/all_to_all | solution.py:86
  50.8 0.0 copy-done.4
  50.8 1.5 fusion.82
  52.4 0.2 reshape.51
  52.5 0.3 multiply_reduce_fusion
  52.9 0.3 multiply_convert_fusion
  53.3 117.9 %all-to-all-done = bf16[32,256,512]{1,2,0:T(8,128)(2,1)} async-done(((bf16[32,256,512]{1,2,0:T(8,128)(2,1)}), bf16[32,256,512]{1,2,0:T(8,128)(2,1)}, u32[]{:S(2)}, u32[]{:S(2)}) %all-to-all-start) | async-done | bytes 8388640 | tf_op jit(solution)/shard_map/all_to_all | solution.py:86
  171.1 11.4 %copy.25 = bf16[32,256,512]{1,0,2:T(8,128)(2,1)} copy(bf16[32,256,512]{1,2,0:T(8,128)(2,1)} %all-to-all-done) | data formatting | bytes 16777216 | tf_op jit(solution)/shard_map/all_to_all | solution.py:86
  182.5 13.4 %reshape.52 = bf16[8192,4,128]{0,2,1:T(8,128)(2,1)} reshape(bf16[32,256,512]{1,0,2:T(8,128)(2,1)} %copy.25) | data formatting | bytes 16777216 | tf_op jit(solution)/shard_map/reshape | solution.py:96
  196.0 16.5 %fusion.101 = (f32[4,256]{1,0:T(4,128)S(1)}, f32[4,256,8192]{2,1,0:T(8,128)}) fusion(bf16[8192,4,128]{0,2,1:T(8,128)(2,1)} %reshape.52, bf16[256,4,128]{2,1,0:T(4,128)(2,1)S(1)} %multiply_convert_fusion), kind=kOutput, calls=%fused_computation.100 | convolution fusion | flops 2155871232 | bytes 42209280 | tf_op jit(solution)/shard_map/thd,shd->hts/dot_general | solution.py:36
  212.5 13.6 %fusion = f32[4,256]{1,0:T(4,128)S(1)} fusion(f32[4,256,8192]{2,1,0:T(8,128)} %get-tuple-element.10, f32[4,256]{1,0:T(4,128)S(1)} %broadcast_maximum_fusion), kind=kLoop, calls=%fused_computation.1 | loop fusion | flops 16776192 | bytes 33562624 | tf_op jit(solution)/shard_map/reduce_sum | solution.py:39
  226.2 0.0 all-gather.2.cloned.1.call-done
  226.2 12.0 %copy.30 = bf16[8192,512]{0,1:T(8,128)(2,1)} copy(bf16[8192,512]{1,0:T(8,128)(2,1)} %all-gather.2.cloned.1.call-done) | data formatting | bytes 16777216 | tf_op jit(solution)/shard_map/reshape | solution.py:97
  238.2 16.0 %fusion.45 = bf16[256,4,128]{0,2,1:T(8,128)(2,1)S(1)} fusion(bf16[8192,4,128]{0,2,1:T(8,128)(2,1)} %bitcast.66, f32[4,256,8192]{2,1,0:T(8,128)} %get-tuple-element.10, f32[4,256]{1,0:T(4,128)S(1)} %broadcast_maximum_fusion, f32[256,4]{0,1:T(4,128)S(1)} %bitcast.71), kind=kOutput, calls=%fused_computation.36 | convolution fusion | flops 2164523008 | bytes 42213376 | tf_op jit(solution)/shard_map/hts,shd->htd/dot_general | solution.py:40
  254.3 0.0 copy-done
  254.3 1.1 fusion.38
  (8 shorter events, 0.1 us)
Async XLA Ops:
  6.5 247.7 %copy-start = (bf16[512,768]{1,0:T(8,128)(2,1)S(1)}, bf16[512,768]{1,0:T(8,128)(2,1)}, u32[]{:S(2)}) copy-start(bf16[512,768]{1,0:T(8,128)(2,1)} %param.10) | copy-start | bytes 2359300
  6.5 219.6 %all-gather.2.cloned.1.call-start = ((), (), s32[]{:S(2)}) async-start(), calls=%async_computation.1 | async-start | bytes 8650752 | tf_op jit(solution)/shard_map/all_gather | solution.py:93
  7.4 8.7 %collective-permute-start.1 = (bf16[2,1536]{1,0:T(2,128)(2,1)S(1)}, bf16[2,1536]{1,0:T(2,128)(2,1)S(1)}, u32[]{:S(2)}, u32[]{:S(2)}) collective-permute-start(bf16[2,1536]{1,0:T(2,128)(2,1)S(1)} %get-tuple-element.6), channel_id=1, source_target_pairs={{4,0},{8,4},{12,8},{16,12},{20,16},{24,20},{28,24},{32,28},{36,32}... | collective-permute-start | bytes 18440 | tf_op jit(solution)/shard_map/ppermute | solution.py:16
  8.7 9.9 %copy-start.3 = (bf16[5,1536,768]{2,1,0:T(8,128)(2,1)S(1)}, bf16[5,1536,768]{2,1,0:T(8,128)(2,1)}, u32[]{:S(2)}) copy-start(bf16[5,1536,768]{2,1,0:T(8,128)(2,1)} %param.7) | copy-start | bytes 35389444
  8.7 10.7 %collective-permute-start = (bf16[2,1536]{1,0:T(2,128)(2,1)S(1)}, bf16[2,1536]{1,0:T(2,128)(2,1)S(1)}, u32[]{:S(2)}, u32[]{:S(2)}) collective-permute-start(bf16[2,1536]{1,0:T(2,128)(2,1)S(1)} %get-tuple-element.5), channel_id=1, source_target_pairs={{0,4},{4,8},{8,12},{12,16},{16,20},{20,24},{24,28},{28,32},{32,36}... | collective-permute-start | bytes 18440 | tf_op jit(solution)/shard_map/ppermute | solution.py:13
  16.0 3.4 %copy-start.2 = (bf16[256,1536]{1,0:T(8,128)(2,1)S(1)}, bf16[256,1536]{1,0:T(8,128)(2,1)}, u32[]{:S(2)}) copy-start(bf16[256,1536]{1,0:T(8,128)(2,1)} %param.6) | copy-start | bytes 2359300
  19.4 5.0 %slice-start = ((s8[5898240]{0:T(1024)(128)(4,1)}), s8[4194304]{0:T(1024)(128)(4,1)S(1)}, s32[]{:S(2)}) async-start(s8[5898240]{0:T(1024)(128)(4,1)} %bitcast.67), calls=%async_computation.2 | async-start | bytes 8388608
  20.2 4.2 %slice-start.1 = ((s8[5898240]{0:T(1024)(128)(4,1)}), s8[1703936]{0:T(1024)(128)(4,1)S(1)}, s32[]{:S(2)}) async-start(s8[5898240]{0:T(1024)(128)(4,1)} %bitcast.67), calls=%async_computation.3 | async-start | bytes 3407872
  21.3 4.9 %collective-permute-start.2 = (bf16[2,768]{1,0:T(2,128)(2,1)S(1)}, bf16[2,768]{1,0:T(2,128)(2,1)S(1)}, u32[]{:S(2)}, u32[]{:S(2)}) collective-permute-start(bf16[2,768]{1,0:T(2,128)(2,1)S(1)} %get-tuple-element.7), channel_id=1, source_target_pairs={{0,4},{4,8},{8,12},{12,16},{16,20},{20,24},{24,28},{28,32},{32,36}... | collective-permute-start | bytes 9224 | tf_op jit(solution)/shard_map/ppermute | solution.py:13
  24.9 3.6 %collective-permute-start.3 = (bf16[2,768]{1,0:T(2,128)(2,1)S(1)}, bf16[2,768]{1,0:T(2,128)(2,1)S(1)}, u32[]{:S(2)}, u32[]{:S(2)}) collective-permute-start(bf16[2,768]{1,0:T(2,128)(2,1)S(1)} %get-tuple-element.8), channel_id=1, source_target_pairs={{4,0},{8,4},{12,8},{16,12},{20,16},{24,20},{28,24},{32,28},{36,32}... | collective-permute-start | bytes 9224 | tf_op jit(solution)/shard_map/ppermute | solution.py:16
  26.7 3.3 %copy-start.1 = (bf16[768,1536]{1,0:T(8,128)(2,1)S(1)}, bf16[768,1536]{1,0:T(8,128)(2,1)}, u32[]{:S(2)}) copy-start(bf16[768,1536]{1,0:T(8,128)(2,1)} %param.9) | copy-start | bytes 7077892
  36.7 14.1 %copy-start.4 = (f32[4]{0:T(128)S(1)}, f32[4]{0:T(128)}, u32[]{:S(2)}) copy-start(f32[4]{0:T(128)} %param.11) | copy-start | bytes 52
  36.7 134.4 %all-to-all-start = ((bf16[32,256,512]{1,2,0:T(8,128)(2,1)}), bf16[32,256,512]{1,2,0:T(8,128)(2,1)}, u32[]{:S(2)}, u32[]{:S(2)}) async-start(bf16[32,256,512]{1,2,0:T(8,128)(2,1)} %tile.2), calls=%async_computation | async-start | bytes 16777216 | tf_op jit(solution)/shard_map/all_to_all | solution.py:86
Sparse Core Ops, SparseCore 0:
  31.5 135.2 all-gather.1
